TPU v7x, 32 devices: a whole 2x2x4 slice. The times are simulated.
32 devices in a mesh: grp: 2 (over y), gene: 4 (over z), cell: 4 (over x, core).
Axes of the slice: x: 2, y: 2, z: 4, core: 2. Of those that a mesh axis runs over, the one named last changes fastest.
Arguments:
- expression: bfloat16 [4096, 32768], P(('grp', 'cell'), 'gene'), parts along dimension 0, may hold values from -6 to 6
- gene_mask: int32 [4096, 32768], P(('grp', 'cell'), 'gene'), parts along dimension 0, may hold values 0 or 1
- mask_value: bfloat16 [32768], P('gene'), may hold values from -4 to 4
- w_qkv: bfloat16 [32768, 3072], P('gene'), may hold values from -0.03125 to 0.03125
- w_out: bfloat16 [1024, 32768], P(None, 'gene'), may hold values from -1.5 to 1.5
- w_first: bfloat16 [128, 256, 256], P('gene'), may hold values from -0.375 to 0.375
- w_second: bfloat16 [128, 256, 256], P('gene'), may hold values from -0.375 to 0.375
- cotangent: bfloat16 [4096, 32768], P(('grp', 'cell'), 'gene'), parts along dimension 0, may hold values from -6 to 6
Outputs:
- denoised: bfloat16 [4096, 32768], P(('grp', 'cell'), 'gene'), parts along dimension 0
- grad_first: float32 [256, 256, 256], P(('grp', 'gene'), 'cell'), parts along dimension 0
- grad_second: float32 [256, 256, 256], P(('grp', 'gene'), 'cell'), parts along dimension 0
There are 2 independent parts, one for each index of `grp`. A program takes and returns all parts, laid end to end along the dimension named above; an argument that names none is the same for every part. Nothing has to cross between parts.
All inputs are finite; a program needn't handle non-finite values. No bound on the sum of `gene_mask` on one device may be relied on, other than what follows from the above.
Results may differ from a plain program's by a relative error of at most 0.02.
Values may be sent and summed in bfloat16 or wider, within the bound.
A program may use at most 256 MiB of HBM per device.

v0:
```python
import jax
import jax.numpy as jnp
from jax import lax
from jax.sharding import PartitionSpec as P

HEADS = 16
HEAD_DIM = 64


def normalize(part):
    count = part.shape[0]
    shaped = part.reshape(count, HEADS, HEAD_DIM)
    meansq = jnp.mean(shaped * shaped, axis=-1, keepdims=True)
    return (
        (shaped * lax.rsqrt(meansq + 1e-06)).astype(jnp.bfloat16).reshape(count, HEADS * HEAD_DIM)
    )


def split_heads(qkv_sums):
    columns = qkv_sums.shape[1] // 3
    queries = normalize(qkv_sums[:, :columns])
    keys_normed = normalize(qkv_sums[:, columns : 2 * columns])
    values_b = qkv_sums[:, 2 * columns :].astype(jnp.bfloat16)
    return (queries, keys_normed, values_b)


def attend(queries, pieces):
    key_piece, value_piece = pieces
    query_count = queries.shape[0]
    key_count = key_piece.shape[0]
    query_heads = queries.reshape(query_count, HEADS, HEAD_DIM)
    key_heads = key_piece.reshape(key_count, HEADS, HEAD_DIM)
    value_heads = value_piece.reshape(key_count, HEADS, HEAD_DIM)
    scores = jnp.einsum(
        "qhd,khd->hqk", query_heads, key_heads, preferred_element_type=jnp.float32
    ) * HEAD_DIM ** (-0.5)
    expw = jnp.exp(scores).astype(jnp.bfloat16)
    denom = jnp.sum(expw, axis=2, dtype=jnp.float32)
    numer = jnp.einsum("hqk,khd->qhd", expw, value_heads, preferred_element_type=jnp.float32)
    return (numer, denom)


def finish(totals):
    numer, denom = totals
    query_count = numer.shape[0]
    return (numer / denom.T[:, :, None]).astype(jnp.bfloat16).reshape(query_count, HEADS * HEAD_DIM)


def on_device(expression, gene_mask, mask_value, w_qkv, w_out, w_first, w_second, cotangent):
    groups = lax.axis_size("gene")
    local_blocks = w_first.shape[0]
    block_size = w_first.shape[1]
    block_total = local_blocks * groups
    cell_rows = expression.shape[0]
    masked_in = jnp.where(gene_mask == 1, mask_value[None, :], expression)
    qkv_part = jnp.dot(masked_in, w_qkv, preferred_element_type=jnp.float32)
    qkv_full = lax.psum(qkv_part.astype(jnp.bfloat16), "gene").astype(jnp.float32)
    queries, keys_normed, values_b = split_heads(qkv_full)
    totals = attend(
        queries,
        (
            lax.all_gather(keys_normed, "cell", axis=0, tiled=True),
            lax.all_gather(values_b, "cell", axis=0, tiled=True),
        ),
    )
    attended = finish(totals)
    added = jnp.dot(attended, w_out, preferred_element_type=jnp.float32)
    hidden = (masked_in.astype(jnp.float32) + added).astype(jnp.bfloat16)
    blocks = hidden.reshape(cell_rows, local_blocks, block_size)
    first = jnp.einsum("cbi,bio->cbo", blocks, w_first, preferred_element_type=jnp.float32).astype(
        jnp.bfloat16
    )
    cot_blocks = cotangent.reshape(cell_rows, local_blocks, block_size)
    back_perm = jnp.einsum(
        "cjo,jko->cjk", cot_blocks, w_second, preferred_element_type=jnp.float32
    ).astype(jnp.bfloat16)
    back_send = back_perm.reshape(cell_rows, block_size // groups, block_total)
    received = lax.all_to_all(first, "gene", split_axis=2, concat_axis=1, tiled=True)
    permuted = jnp.swapaxes(received, 1, 2).reshape(cell_rows, local_blocks, block_size)
    mixed = jnp.einsum("cjk,jko->cjo", permuted, w_second, preferred_element_type=jnp.float32)
    denoised = (
        (blocks.astype(jnp.float32) + mixed)
        .astype(jnp.bfloat16)
        .reshape(cell_rows, local_blocks * block_size)
    )
    grad_second = jnp.einsum(
        "cjk,cjo->jko", permuted, cot_blocks, preferred_element_type=jnp.float32
    )
    back_recv = lax.all_to_all(back_send, "gene", split_axis=2, concat_axis=1, tiled=True)
    back_first = jnp.swapaxes(back_recv, 1, 2)
    grad_first = jnp.einsum("cbi,cbo->bio", blocks, back_first, preferred_element_type=jnp.float32)
    first_share, second_share = (
        lax.psum_scatter(
            grad_first.astype(jnp.bfloat16), "cell", scatter_dimension=1, tiled=True
        ).astype(jnp.float32),
        lax.psum_scatter(
            grad_second.astype(jnp.bfloat16), "cell", scatter_dimension=1, tiled=True
        ).astype(jnp.float32),
    )
    return (denoised, first_share, second_share)


def solution(mesh):
    placed = (
        P(("grp", "cell"), "gene"),
        P(("grp", "cell"), "gene"),
        P("gene"),
        P("gene", None),
        P(None, "gene"),
        P("gene", None, None),
        P("gene", None, None),
        P(("grp", "cell"), "gene"),
    )
    return jax.shard_map(
        on_device,
        mesh=mesh,
        in_specs=placed,
        out_specs=(
            P(("grp", "cell"), "gene"),
            P(("grp", "gene"), "cell", None),
            P(("grp", "gene"), "cell", None),
        ),
        check_vma=False,
    )
```

profile of v0, /device:TPU:0, one launch (start us, length us, event | category | flops | bytes accessed | tf_op | source)
XLA Modules:
  0.0 680.1 jit_solution(10328082861231233537)
XLA Ops:
  7.2 9.0 %compare_select_fusion = bf16[512,8192]{1,0:T(8,128)(2,1)S(1)} fusion(bf16[512,8192]{1,0:T(8,128)(2,1)} %param.8, s32[512,8192]{1,0:T(8,128)} %param.9, bf16[8192]{0:T(1024)(128)(2,1)} %param.10), kind=kLoop, calls=%fused_computation.5 | loop fusion | flops 8388608 | bytes 33570816 | tf_op jit(solution)/shard_map/jit(_where)/select_n | solution.py:55
  16.3 3.4 copy-done
  19.7 32.1 %convolution_convert_fusion = bf16[512,3072]{1,0:T(8,128)(2,1)} fusion(bf16[512,8192]{1,0:T(8,128)(2,1)S(1)} %compare_select_fusion, bf16[8192,3072]{1,0:T(8,128)(2,1)} %param.11), kind=kOutput, calls=%fused_computation.16 | convolution fusion | flops 25771376640 | bytes 61865984 | tf_op jit(solution)/shard_map/dot_general | solution.py:56
  51.9 123.9 %all-reduce.2.cloned.1.call-done = bf16[512,3072]{1,0:T(8,128)(2,1)} async-done(((bf16[512,3072]{1,0:T(8,128)(2,1)}), bf16[512,3072]{1,0:T(8,128)(2,1)}) %all-reduce.2.cloned.1.call-update) | async-done | bytes 3145744 | tf_op jit(solution)/shard_map/psum | solution.py:57
  186.7 2.9 copy.62
  189.6 3.5 multiply_convert_fusion
  194.4 10.6 %fusion.9 = bf16[32,256,512]{2,1,0:T(8,128)(2,1)} fusion(bf16[32,256,256]{2,1,0:T(8,128)(2,1)} %param.14, bf16[64,32,8,256]{3,2,1,0:T(8,128)(2,1)} %bitcast.75), kind=kOutput, calls=%fused_computation.15 | convolution fusion | flops 2151677952 | bytes 20971520 | tf_op jit(solution)/shard_map/cjo,jko->cjk/dot_general | solution.py:74
  205.0 11.4 %copy.73 = bf16[512,64,128]{0,1,2:T(8,128)(2,1)} copy(bf16[512,64,128]{0,2,1:T(8,128)(2,1)} %bitcast.72) | data formatting | bytes 16777216 | tf_op jit(solution)/shard_map/reshape | solution.py:77
  216.4 5.8 all-to-all-start.1
  226.8 6.5 copy.63
  233.3 30.1 %all-gather.3.cloned.1.call-done = bf16[2048,1024]{1,0:T(8,128)(2,1)} async-done(((bf16[512,1024]{1,0:T(8,128)(2,1)}), bf16[2048,1024]{1,0:T(8,128)(2,1)}) %all-gather.3.cloned.1.call-update) | async-done | bytes 4194320 | tf_op jit(solution)/shard_map/all_gather | solution.py:63
  263.4 6.5 copy.59
  269.9 18.0 %convert_reduce_fusion = (f32[16,512]{1,0:T(8,128)S(1)}, bf16[16,512,2048]{2,1,0:T(8,128)(2,1)}) fusion(bf16[2048,16,64]{0,2,1:T(8,128)(2,1)} %bitcast.79, f32[512,16,64]{0,2,1:T(8,128)S(1)} %bitcast.77, f32[512,16]{0,1:T(8,128)S(1)} %add_rsqrt_fusion.1), kind=kOutput, calls=%fused_computation | convolution fusion | flops 2215632896 | bytes 39911424 | tf_op jit(solution)/shard_map/qhd,khd->hqk/dot_general | solution.py:34
  287.9 17.0 %fusion.18 = bf16[512,16,64]{0,2,1:T(8,128)(2,1)S(1)} fusion(bf16[2048,16,64]{0,2,1:T(8,128)(2,1)} %bitcast.73, bf16[16,512,2048]{2,1,0:T(8,128)(2,1)} %get-tuple-element.16, f32[512,16]{0,1:T(8,128)S(1)} %bitcast.80), kind=kOutput, calls=%fused_computation.20 | convolution fusion | flops 2148532224 | bytes 38830080 | tf_op jit(solution)/shard_map/hqk,khd->qhd/dot_general | solution.py:39
  304.9 18.4 %add_convert_fusion = bf16[512,8192]{1,0:T(8,128)(2,1)} fusion(bf16[512,8192]{1,0:T(8,128)(2,1)} %copy-done, bf16[512,1024]{0,1:T(8,128)(2,1)S(1)} %bitcast.74, bf16[1024,8192]{1,0:T(8,128)(2,1)} %param.12), kind=kOutput, calls=%fused_computation.4 | convolution fusion | flops 8602517504 | bytes 34603008 | tf_op jit(solution)/shard_map/dot_general | solution.py:67
  323.3 12.0 %copy.84 = bf16[512,8192]{0,1:T(8,128)(2,1)} copy(bf16[512,8192]{1,0:T(8,128)(2,1)} %add_convert_fusion) | data formatting | bytes 16777216 | tf_op jit(solution)/shard_map/reshape | solution.py:69
  335.3 8.6 %convert_bitcast_fusion = bf16[512,32,256]{2,0,1:T(8,128)(2,1)} fusion(bf16[512,32,256]{0,2,1:T(8,128)(2,1)} %bitcast.64, bf16[32,256,256]{2,1,0:T(8,128)(2,1)} %param.13), kind=kOutput, calls=%fused_computation.12 | convolution fusion | flops 2151677952 | bytes 20971520 | tf_op jit(solution)/shard_map/cbi,bio->cbo/dot_general | solution.py:70
  343.9 14.7 %copy.66 = bf16[512,32,256]{0,1,2:T(8,128)(2,1)} copy(bf16[512,32,256]{2,0,1:T(8,128)(2,1)} %convert_bitcast_fusion) | data formatting | bytes 16777216 | tf_op jit(solution)/shard_map/convert_element_type | solution.py:70
  358.6 46.8 %all-to-all-done.1 = bf16[512,64,128]{0,1,2:T(8,128)(2,1)} async-done(((bf16[512,64,128]{0,1,2:T(8,128)(2,1)}), bf16[512,64,128]{0,1,2:T(8,128)(2,1)}, u32[]{:S(2)}, u32[]{:S(2)}) %all-to-all-start.1) | async-done | bytes 8388640 | tf_op jit(solution)/shard_map/all_to_all | solution.py:89
  405.4 5.6 all-to-all-start
  411.1 11.6 %copy.75 = bf16[512,4,64,32]{0,3,2,1:T(8,128)(2,1)} copy(bf16[512,4,64,32]{0,2,3,1:T(8,128)(2,1)} %bitcast.21) | data formatting | bytes 16777216 | tf_op jit(solution)/shard_map/all_to_all | solution.py:89
  422.7 13.7 %copy.76 = bf16[512,256,32]{1,0,2:T(8,128)(2,1)} copy(bf16[512,256,32]{0,2,1:T(8,128)(2,1)} %bitcast.70) | data formatting | bytes 16777216 | tf_op jit(solution)/shard_map/all_to_all | solution.py:89
  436.4 10.2 %fusion.12 = bf16[32,256,256]{2,1,0:T(8,128)(2,1)} fusion(bf16[512,32,256]{0,2,1:T(8,128)(2,1)} %bitcast.65, bf16[512,256,32]{1,0,2:T(8,128)(2,1)} %copy.76), kind=kOutput, calls=%fused_computation.17 | convolution fusion | flops 2149580800 | bytes 20971520 | tf_op jit(solution)/shard_map/cbi,cbo->bio/dot_general | solution.py:91
  446.8 146.8 %all-to-all-done = bf16[512,32,256]{0,1,2:T(8,128)(2,1)} async-done(((bf16[512,32,256]{0,1,2:T(8,128)(2,1)}), bf16[512,32,256]{0,1,2:T(8,128)(2,1)}, u32[]{:S(2)}, u32[]{:S(2)}) %all-to-all-start) | async-done | bytes 8388640 | tf_op jit(solution)/shard_map/all_to_all | solution.py:78
  593.6 11.6 %copy.68 = bf16[512,4,32,64]{0,3,2,1:T(8,128)(2,1)} copy(bf16[512,4,32,64]{0,2,3,1:T(8,128)(2,1)} %bitcast.11) | data formatting | bytes 16777216 | tf_op jit(solution)/shard_map/all_to_all | solution.py:78
  605.3 11.3 %copy.69 = bf16[512,64,128]{0,2,1:T(8,128)(2,1)} copy(bf16[512,64,128]{0,1,2:T(8,128)(2,1)} %bitcast.71) | data formatting | bytes 16777216 | tf_op jit(solution)/shard_map/transpose | solution.py:79
  616.6 10.3 %fusion.15 = bf16[32,256,256]{2,1,0:T(8,128)(2,1)} fusion(bf16[512,32,256]{0,2,1:T(8,128)(2,1)} %bitcast.67, bf16[64,32,8,256]{3,2,1,0:T(8,128)(2,1)} %bitcast.76), kind=kOutput, calls=%fused_computation.18 | convolution fusion | flops 2149580800 | bytes 20971520 | tf_op jit(solution)/shard_map/cjk,cjo->jko/dot_general | solution.py:86
  627.0 2.8 convert_element_type.75
  629.8 12.9 %fusion = bf16[512,32,256]{0,2,1:T(8,128)(2,1)} fusion(bf16[512,32,256]{0,2,1:T(8,128)(2,1)} %bitcast.66, bf16[512,32,256]{0,2,1:T(8,128)(2,1)} %bitcast.68, bf16[32,256,256]{2,1,0:T(8,128)(2,1)} %param.14), kind=kOutput, calls=%fused_computation.3 | convolution fusion | flops 2160066560 | bytes 29360128 | tf_op jit(solution)/shard_map/cjk,jko->cjo/dot_general | solution.py:80
  642.6 12.0 %copy.79 = bf16[512,8192]{1,0:T(8,128)(2,1)} copy(bf16[512,8192]{0,1:T(8,128)(2,1)} %bitcast.69) | data formatting | bytes 16777216
  654.6 16.0 %reduce-scatter.5.cloned.1.call-done = bf16[32,64,256]{2,1,0:T(8,128)(2,1)} async-done(((bf16[32,256,256]{2,1,0:T(8,128)(2,1)}), bf16[32,64,256]{2,1,0:T(8,128)(2,1)}) %reduce-scatter.5.cloned.1.call-update) | async-done | bytes 1048592 | tf_op jit(solution)/shard_map/reduce_scatter | solution.py:96
  670.6 2.8 convert_element_type.77
  (28 shorter events, 17.1 us)
Async XLA Ops:
  7.2 168.6 %all-reduce.2.cloned.1.call-start = ((), (), s32[]{:S(2)}) async-start(), calls=%async_computation.4 | async-start | bytes 6291456 | tf_op jit(solution)/shard_map/psum | solution.py:57
  16.3 3.4 copy-start
  51.8 175.0 %all-gather.5.cloned.1.call-start = ((), (), s32[]{:S(2)}) async-start(), calls=%async_computation.6 | async-start | bytes 5242880 | tf_op jit(solution)/shard_map/all_gather | solution.py:62
  178.4 2.7 copy-start.1
  183.1 10.3 %copy-start.2 = (bf16[512,3072]{1,0:T(8,128)(2,1)S(1)}, bf16[512,3072]{1,0:T(8,128)(2,1)}, u32[]{:S(2)}) copy-start(bf16[512,3072]{1,0:T(8,128)(2,1)} %all-reduce.2.cloned.1.call-done) | copy-start | bytes 9437188
  193.1 70.3 %all-gather.3.cloned.1.call-start = ((), (), s32[]{:S(2)}) async-start(), calls=%async_computation.5 | async-start | bytes 5242880 | tf_op jit(solution)/shard_map/all_gather | solution.py:63
  216.4 189.0 %all-to-all-start.1 = ((bf16[512,64,128]{0,1,2:T(8,128)(2,1)}), bf16[512,64,128]{0,1,2:T(8,128)(2,1)}, u32[]{:S(2)}, u32[]{:S(2)}) async-start(bf16[512,64,128]{0,1,2:T(8,128)(2,1)} %copy.73), calls=%async_computation.1 | async-start | bytes 16777216 | tf_op jit(solution)/shard_map/all_to_all | solution.py:89
  405.4 188.3 %all-to-all-start = ((bf16[512,32,256]{0,1,2:T(8,128)(2,1)}), bf16[512,32,256]{0,1,2:T(8,128)(2,1)}, u32[]{:S(2)}, u32[]{:S(2)}) async-start(bf16[512,32,256]{0,1,2:T(8,128)(2,1)} %copy.66), calls=%async_computation | async-start | bytes 16777216 | tf_op jit(solution)/shard_map/all_to_all | solution.py:78
  411.0 215.9 %reduce-scatter.3.cloned.1.call-start = ((), (), s32[]{:S(2)}) async-start(), calls=%async_computation.7 | async-start | bytes 5242880 | tf_op jit(solution)/shard_map/reduce_scatter | solution.py:93
  446.6 223.9 %reduce-scatter.5.cloned.1.call-start = ((), (), s32[]{:S(2)}) async-start(), calls=%async_computation.8 | async-start | bytes 5242880 | tf_op jit(solution)/shard_map/reduce_scatter | solution.py:96
Sparse Core Ops, SparseCore 0:
  51.9 123.7 all-reduce.1
  193.3 33.4 all-gather.4
  228.9 34.4 all-gather.2
  446.7 45.7 reduce-scatter.2
  627.0 43.4 reduce-scatter.4
where the time goes:
time: 688 us; the launch traced here: 680 us
  waiting for transfers between devices  364 us (53%)
  matrix products  138 us (20%)
  local copies, waits for them, and re-layouts  128 us (19%)
  other arithmetic  23.4 us (3%)
  between operations  14.1 us (2%)
  starting transfers between devices  12 us (2%)
    all_to_all x1, waiting for transfers between devices, on_device(): lax.all_to_all(first, 'gene', split_axis=2, concat_axis=1, tiled=True)  147 us
    psum x1, waiting for transfers between devices, on_device(): lax.psum(qkv_part.astype(jnp.bfloat16), 'gene').astype(jnp.float32)  124 us
    all_to_all x1, waiting for transfers between devices, on_device(): lax.all_to_all(back_send, 'gene', split_axis=2, concat_axis=1, tiled=True)  46.8 us
    dot_general x1, matrix products, on_device(): qkv_part = jnp.dot(masked_in, w_qkv, preferred_element_type=jnp.float32)  32.1 us
    all_gather x1, waiting for transfers between devices, on_device(): lax.all_gather(values_b, 'cell', axis=0, tiled=True)  30.1 us
    all_to_all x2, local copies, waits for them, and re-layouts, on_device(): lax.all_to_all(back_send, 'gene', split_axis=2, concat_axis=1, tiled=True)  25.3 us
    dot_general x1, matrix products, on_device(): added = jnp.dot(attended, w_out, preferred_element_type=jnp.float32)  18.4 us
    unnamed x7, local copies, waits for them, and re-layouts  18 us
  transfers between devices with their start and end apart: 7, of which 6 were waited for; matrix products, arithmetic and copies ran while one was open for 33% of the time, Pallas kernels for 0%

commit v1 on v0

--- a/solution.py
+++ b/solution.py
@@ -86,7 +86,10 @@
     grad_second = jnp.einsum(
         "cjk,cjo->jko", permuted, cot_blocks, preferred_element_type=jnp.float32
     )
-    back_recv = lax.all_to_all(back_send, "gene", split_axis=2, concat_axis=1, tiled=True)
+    size = lax.axis_size("gene")
+    tiles = jnp.stack(jnp.split(back_send, size, axis=2), axis=0)
+    tiles = lax.all_to_all(tiles, "gene", split_axis=0, concat_axis=0)
+    back_recv = jnp.concatenate(tiles, axis=1)
     back_first = jnp.swapaxes(back_recv, 1, 2)
     grad_first = jnp.einsum("cbi,cbo->bio", blocks, back_first, preferred_element_type=jnp.float32)
     first_share, second_share = (

time: 688 us -> 696 us (1.012)
  local copies, waits for them, and re-layouts: 128 us -> 109 us
  waiting for transfers between devices: 364 us -> 376 us
  starting transfers between devices: 12 us -> 22.7 us
    all_to_all x2 -> x0, local copies, waits for them, and re-layouts: 25.3 us -> none  [on_device(): lax.all_to_all(back_send, 'gene', split_axis=2, concat_axis=1, tiled=True)]
    all_to_all x1, waiting for transfers between devices: 147 us -> 159 us  [on_device(): lax.all_to_all(first, 'gene', split_axis=2, concat_axis=1, tiled=True)]
    all_to_all x1, starting transfers between devices: 5.84 us -> 16.7 us  [on_device(): tiles = lax.all_to_all(tiles, 'gene', split_axis=0, concat_axis=0)]
    all_to_all x1, waiting for transfers between devices: 46.8 us -> 54.5 us  [on_device(): tiles = lax.all_to_all(tiles, 'gene', split_axis=0, concat_axis=0)]
  transfers between devices with their start and end apart: 7 -> 7, of which waited for: 6 -> 5; matrix products, arithmetic and copies ran while one was open for 33% -> 31% of each run, Pallas kernels for 0% -> 0%
where the time goes in v1:
time: 696 us; the launch traced here: 686 us
  waiting for transfers between devices  376 us (54%)
  matrix products  138 us (20%)
  local copies, waits for them, and re-layouts  109 us (16%)
  other arithmetic  26.2 us (4%)
  starting transfers between devices  22.7 us (3%)
  between operations  14.4 us (2%)
    all_to_all x1, waiting for transfers between devices, on_device(): lax.all_to_all(first, 'gene', split_axis=2, concat_axis=1, tiled=True)  159 us
    psum x1, waiting for transfers between devices, on_device(): lax.psum(qkv_part.astype(jnp.bfloat16), 'gene').astype(jnp.float32)  124 us
    all_to_all x1, waiting for transfers between devices, on_device(): tiles = lax.all_to_all(tiles, 'gene', split_axis=0, concat_axis=0)  54.5 us
    dot_general x1, matrix products, on_device(): qkv_part = jnp.dot(masked_in, w_qkv, preferred_element_type=jnp.float32)  32.2 us
    all_gather x1, waiting for transfers between devices, on_device(): lax.all_gather(values_b, 'cell', axis=0, tiled=True)  23.4 us
    dot_general x1, matrix products, on_device(): added = jnp.dot(attended, w_out, preferred_element_type=jnp.float32)  18.4 us
    unnamed x7, local copies, waits for them, and re-layouts  18 us
    dot_general x1, matrix products, attend(): jnp.einsum('qhd,khd->hqk', query_heads, key_heads, preferred_element_type...  18 us
  transfers between devices with their start and end apart: 7, of which 5 were waited for; matrix products, arithmetic and copies ran while one was open for 31% of the time, Pallas kernels for 0%

profile of v1, /device:TPU:0, one launch (start us, length us, event | category | flops | bytes accessed | tf_op | source)
XLA Modules:
  0.0 686.1 jit_solution(11831191989982655681)
XLA Ops:
  7.2 9.0 %compare_select_fusion = bf16[512,8192]{1,0:T(8,128)(2,1)S(1)} fusion(bf16[512,8192]{1,0:T(8,128)(2,1)} %param.8, s32[512,8192]{1,0:T(8,128)} %param.9, bf16[8192]{0:T(1024)(128)(2,1)} %param.10), kind=kLoop, calls=%fused_computation.5 | loop fusion | flops 8388608 | bytes 33570816 | tf_op jit(solution)/shard_map/jit(_where)/select_n | solution.py:55
  16.3 3.4 copy-done
  19.7 32.2 %convolution_convert_fusion = bf16[512,3072]{1,0:T(8,128)(2,1)} fusion(bf16[512,8192]{1,0:T(8,128)(2,1)S(1)} %compare_select_fusion, bf16[8192,3072]{1,0:T(8,128)(2,1)} %param.11), kind=kOutput, calls=%fused_computation.17 | convolution fusion | flops 25771376640 | bytes 61865984 | tf_op jit(solution)/shard_map/dot_general | solution.py:56
  51.9 123.9 %all-reduce.2.cloned.1.call-done = bf16[512,3072]{1,0:T(8,128)(2,1)} async-done(((bf16[512,3072]{1,0:T(8,128)(2,1)}), bf16[512,3072]{1,0:T(8,128)(2,1)}) %all-reduce.2.cloned.1.call-update) | async-done | bytes 3145744 | tf_op jit(solution)/shard_map/psum | solution.py:57
  175.8 2.7 convert_element_type.61
  188.5 2.9 multiply_convert_fusion
  191.4 10.6 %fusion.9 = bf16[32,256,512]{2,1,0:T(8,128)(2,1)} fusion(bf16[32,256,256]{2,1,0:T(8,128)(2,1)} %param.14, bf16[64,32,8,256]{3,2,1,0:T(8,128)(2,1)} %bitcast.81), kind=kOutput, calls=%fused_computation.16 | convolution fusion | flops 2151677952 | bytes 20971520 | tf_op jit(solution)/shard_map/cjo,jko->cjk/dot_general | solution.py:74
  203.1 4.1 slice_bitcast_fusion.3
  207.2 3.8 pad_maximum_fusion
  211.0 16.7 %all-to-all-start.1 = ((bf16[4,512,64,32]{1,3,2,0:T(8,128)(2,1)}), bf16[4,512,64,32]{1,3,2,0:T(8,128)(2,1)}, u32[]{:S(2)}, u32[]{:S(2)}) async-start(bf16[4,512,64,32]{1,3,2,0:T(8,128)(2,1)} %pad_maximum_fusion), calls=%async_computation.1 | async-start | bytes 16777216 | tf_op jit(solution)/shard_map/all_to_all | solution.py:91
  231.6 6.7 copy.45
  238.3 23.4 %all-gather.3.cloned.1.call-done = bf16[2048,1024]{1,0:T(8,128)(2,1)} async-done(((bf16[512,1024]{1,0:T(8,128)(2,1)}), bf16[2048,1024]{1,0:T(8,128)(2,1)}) %all-gather.3.cloned.1.call-update) | async-done | bytes 4194320 | tf_op jit(solution)/shard_map/all_gather | solution.py:63
  261.7 6.5 copy.41
  268.2 18.0 %convert_reduce_fusion = (f32[16,512]{1,0:T(8,128)S(1)}, bf16[16,512,2048]{2,1,0:T(8,128)(2,1)}) fusion(bf16[2048,16,64]{0,2,1:T(8,128)(2,1)} %bitcast.85, f32[512,16,64]{0,2,1:T(8,128)S(1)} %bitcast.83, f32[512,16]{0,1:T(8,128)S(1)} %add_rsqrt_fusion.1), kind=kOutput, calls=%fused_computation | convolution fusion | flops 2215632896 | bytes 39911424 | tf_op jit(solution)/shard_map/qhd,khd->hqk/dot_general | solution.py:34
  286.1 17.0 %fusion.18 = bf16[512,16,64]{0,2,1:T(8,128)(2,1)S(1)} fusion(bf16[2048,16,64]{0,2,1:T(8,128)(2,1)} %bitcast.79, bf16[16,512,2048]{2,1,0:T(8,128)(2,1)} %get-tuple-element.17, f32[512,16]{0,1:T(8,128)S(1)} %bitcast.86), kind=kOutput, calls=%fused_computation.25 | convolution fusion | flops 2148532224 | bytes 38830080 | tf_op jit(solution)/shard_map/hqk,khd->qhd/dot_general | solution.py:39
  303.2 18.4 %add_convert_fusion = bf16[512,8192]{1,0:T(8,128)(2,1)} fusion(bf16[512,8192]{1,0:T(8,128)(2,1)} %copy-done, bf16[512,1024]{0,1:T(8,128)(2,1)S(1)} %bitcast.80, bf16[1024,8192]{1,0:T(8,128)(2,1)} %param.12), kind=kOutput, calls=%fused_computation.4 | convolution fusion | flops 8602517504 | bytes 34603008 | tf_op jit(solution)/shard_map/dot_general | solution.py:67
  321.6 12.0 %copy.62 = bf16[512,8192]{0,1:T(8,128)(2,1)} copy(bf16[512,8192]{1,0:T(8,128)(2,1)} %add_convert_fusion) | data formatting | bytes 16777216 | tf_op jit(solution)/shard_map/reshape | solution.py:69
  333.6 8.2 %convert_bitcast_fusion = bf16[512,32,256]{2,0,1:T(8,128)(2,1)} fusion(bf16[512,32,256]{0,2,1:T(8,128)(2,1)} %bitcast.71, bf16[32,256,256]{2,1,0:T(8,128)(2,1)} %param.13), kind=kOutput, calls=%fused_computation.13 | convolution fusion | flops 2151677952 | bytes 20971520 | tf_op jit(solution)/shard_map/cbi,bio->cbo/dot_general | solution.py:70
  341.8 14.7 %copy.48 = bf16[512,32,256]{0,1,2:T(8,128)(2,1)} copy(bf16[512,32,256]{2,0,1:T(8,128)(2,1)} %convert_bitcast_fusion) | data formatting | bytes 16777216 | tf_op jit(solution)/shard_map/convert_element_type | solution.py:70
  356.4 54.5 %all-to-all-done.1 = bf16[4,512,64,32]{1,3,2,0:T(8,128)(2,1)} async-done(((bf16[4,512,64,32]{1,3,2,0:T(8,128)(2,1)}), bf16[4,512,64,32]{1,3,2,0:T(8,128)(2,1)}, u32[]{:S(2)}, u32[]{:S(2)}) %all-to-all-start.1) | async-done | bytes 8388640 | tf_op jit(solution)/shard_map/all_to_all | solution.py:91
  410.9 5.7 all-to-all-start
  416.6 13.7 %copy.55 = bf16[512,256,32]{1,0,2:T(8,128)(2,1)} copy(bf16[512,256,32]{0,2,1:T(8,128)(2,1)} %bitcast.25) | data formatting | bytes 16777216 | tf_op jit(solution)/shard_map/reshape | solution.py:92
  430.3 10.0 %fusion.12 = bf16[32,256,256]{2,1,0:T(8,128)(2,1)} fusion(bf16[512,32,256]{0,2,1:T(8,128)(2,1)} %bitcast.72, bf16[512,256,32]{1,0,2:T(8,128)(2,1)} %copy.55), kind=kOutput, calls=%fused_computation.18 | convolution fusion | flops 2149580800 | bytes 20971520 | tf_op jit(solution)/shard_map/cbi,cbo->bio/dot_general | solution.py:94
  440.6 158.6 %all-to-all-done = bf16[512,32,256]{0,1,2:T(8,128)(2,1)} async-done(((bf16[512,32,256]{0,1,2:T(8,128)(2,1)}), bf16[512,32,256]{0,1,2:T(8,128)(2,1)}, u32[]{:S(2)}, u32[]{:S(2)}) %all-to-all-start) | async-done | bytes 8388640 | tf_op jit(solution)/shard_map/all_to_all | solution.py:78
  599.2 11.6 %copy.50 = bf16[512,4,32,64]{0,3,2,1:T(8,128)(2,1)} copy(bf16[512,4,32,64]{0,2,3,1:T(8,128)(2,1)} %bitcast.11) | data formatting | bytes 16777216 | tf_op jit(solution)/shard_map/all_to_all | solution.py:78
  610.8 11.3 %copy.51 = bf16[512,64,128]{0,2,1:T(8,128)(2,1)} copy(bf16[512,64,128]{0,1,2:T(8,128)(2,1)} %bitcast.78) | data formatting | bytes 16777216 | tf_op jit(solution)/shard_map/transpose | solution.py:79
  622.2 10.4 %fusion.15 = bf16[32,256,256]{2,1,0:T(8,128)(2,1)} fusion(bf16[512,32,256]{0,2,1:T(8,128)(2,1)} %bitcast.74, bf16[64,32,8,256]{3,2,1,0:T(8,128)(2,1)} %bitcast.82), kind=kOutput, calls=%fused_computation.19 | convolution fusion | flops 2149580800 | bytes 20971520 | tf_op jit(solution)/shard_map/cjk,cjo->jko/dot_general | solution.py:86
  632.6 2.8 convert_element_type.75
  635.4 13.0 %fusion = bf16[512,32,256]{0,2,1:T(8,128)(2,1)} fusion(bf16[512,32,256]{0,2,1:T(8,128)(2,1)} %bitcast.73, bf16[512,32,256]{0,2,1:T(8,128)(2,1)} %bitcast.75, bf16[32,256,256]{2,1,0:T(8,128)(2,1)} %param.14), kind=kOutput, calls=%fused_computation.3 | convolution fusion | flops 2160066560 | bytes 29360128 | tf_op jit(solution)/shard_map/cjk,jko->cjo/dot_general | solution.py:80
  648.4 12.0 %copy.58 = bf16[512,8192]{1,0:T(8,128)(2,1)} copy(bf16[512,8192]{0,1:T(8,128)(2,1)} %bitcast.76) | data formatting | bytes 16777216
  660.3 16.0 %reduce-scatter.5.cloned.1.call-done = bf16[32,64,256]{2,1,0:T(8,128)(2,1)} async-done(((bf16[32,256,256]{2,1,0:T(8,128)(2,1)}), bf16[32,64,256]{2,1,0:T(8,128)(2,1)}) %reduce-scatter.5.cloned.1.call-update) | async-done | bytes 1048592 | tf_op jit(solution)/shard_map/reduce_scatter | solution.py:99
  676.3 2.8 convert_element_type.77
  (28 shorter events, 15.3 us)
Async XLA Ops:
  7.2 168.6 %all-reduce.2.cloned.1.call-start = ((), (), s32[]{:S(2)}) async-start(), calls=%async_computation.4 | async-start | bytes 6291456 | tf_op jit(solution)/shard_map/psum | solution.py:57
  16.3 3.4 copy-start
  51.9 179.7 %all-gather.5.cloned.1.call-start = ((), (), s32[]{:S(2)}) async-start(), calls=%async_computation.6 | async-start | bytes 5242880 | tf_op jit(solution)/shard_map/all_gather | solution.py:62
  178.5 2.7 copy-start.1
  191.4 70.3 %all-gather.3.cloned.1.call-start = ((), (), s32[]{:S(2)}) async-start(), calls=%async_computation.5 | async-start | bytes 5242880 | tf_op jit(solution)/shard_map/all_gather | solution.py:63
  191.4 10.6 %copy-start.2 = (bf16[512,3072]{1,0:T(8,128)(2,1)S(1)}, bf16[512,3072]{1,0:T(8,128)(2,1)}, u32[]{:S(2)}) copy-start(bf16[512,3072]{1,0:T(8,128)(2,1)} %all-reduce.2.cloned.1.call-done) | copy-start | bytes 9437188
  211.0 199.9 %all-to-all-start.1 = ((bf16[4,512,64,32]{1,3,2,0:T(8,128)(2,1)}), bf16[4,512,64,32]{1,3,2,0:T(8,128)(2,1)}, u32[]{:S(2)}, u32[]{:S(2)}) async-start(bf16[4,512,64,32]{1,3,2,0:T(8,128)(2,1)} %pad_maximum_fusion), calls=%async_computation.1 | async-start | bytes 16777216 | tf_op jit(solution)/shard_map/all_to_all | solution.py:91
  410.9 188.3 %all-to-all-start = ((bf16[512,32,256]{0,1,2:T(8,128)(2,1)}), bf16[512,32,256]{0,1,2:T(8,128)(2,1)}, u32[]{:S(2)}, u32[]{:S(2)}) async-start(bf16[512,32,256]{0,1,2:T(8,128)(2,1)} %copy.48), calls=%async_computation | async-start | bytes 16777216 | tf_op jit(solution)/shard_map/all_to_all | solution.py:78
  416.6 216.0 %reduce-scatter.3.cloned.1.call-start = ((), (), s32[]{:S(2)}) async-start(), calls=%async_computation.7 | async-start | bytes 5242880 | tf_op jit(solution)/shard_map/reduce_scatter | solution.py:96
  440.4 235.9 %reduce-scatter.5.cloned.1.call-start = ((), (), s32[]{:S(2)}) async-start(), calls=%async_computation.8 | async-start | bytes 5242880 | tf_op jit(solution)/shard_map/reduce_scatter | solution.py:99
Sparse Core Ops, SparseCore 0:
  52.0 123.7 all-reduce.1
  191.5 33.4 all-gather.4
  227.2 34.4 all-gather.2
  440.5 45.8 reduce-scatter.2
  632.7 43.5 reduce-scatter.4
